TPU v7x, 256 devices: a whole 4x4x8 slice. The times are simulated.
256 devices in a mesh: narrow: 8 (over x, z_lo), wide: 32 (over y, z_hi, core).
Axes of the slice: x: 4, y: 4, z: 8 (z_hi: 4, z_lo: 2; z = z_hi * 2 + z_lo), core: 2. Of those that a mesh axis runs over, the one named last changes fastest.
Arguments:
- basis: bfloat16 [128, 32, 512, 128], P(None, 'narrow', 'wide'), may hold values from -6 to 6
- rhs: bfloat16 [32, 512, 128], P('narrow', 'wide'), may hold values from -48 to 48
- coeffs: float32 [4, 32, 512, 128], P(None, 'narrow', 'wide'), may hold values from 0.25 to 4
- rows: int32 [4, 32, 512, 128], P(None, 'narrow', 'wide'), may hold values from 0 to 255
- signs: int32 [4, 32, 512, 128], P(None, 'narrow', 'wide'), may hold values from 0 to 1
- params: float32 [256, 4], P(('narrow', 'wide')), may hold values from 0.25 to 4
- order: int32 [256], replicated, may hold values from 0 to 255, each once
Outputs:
- fields: bfloat16 [256, 32, 512, 128], P(None, 'narrow', 'wide')
Inputs may be any that keep to these rules, and one draw needn't show every extreme that they name: `order`: each point number appears exactly once.
All inputs are finite; a program needn't handle non-finite values.
Results may differ from a plain program's by a relative error of at most 0.0056.
Values may be sent and summed in bfloat16 or wider, within the bound.
No kernel may reach another device: no remote copies, remote signals or barrier semaphores. Data moves between devices by JAX's collectives and lax.ppermute only.
A program may use at most 64 MiB of HBM per device.

v0:
```python
import jax
import jax.numpy as jnp
from jax import lax
from jax.sharding import PartitionSpec as P

K = 128
M = 1024
TERMS = 4
NNZ = 4


def extended(cells, sides, width):
    for axis, dim in sides:
        count = lax.axis_size(axis)
        ends = count - 1
        head = lax.slice_in_dim(cells, 0, width, axis=dim)
        tail = lax.slice_in_dim(cells, cells.shape[dim] - width, cells.shape[dim], axis=dim)
        cells = jnp.concatenate(
            [
                lax.ppermute(tail, axis, [(i, (i + 1) % count) for i in range(ends)]),
                cells,
                lax.ppermute(head, axis, [((i + 1) % count, i) for i in range(ends)]),
            ],
            axis=dim,
        )
    return cells


def column_products(sketched, sketched_rhs):
    dims = (((0,), (0,)), ((), ()))
    gram_matrix = lax.dot_general(
        sketched,
        sketched,
        dims,
        precision=lax.Precision.HIGHEST,
        preferred_element_type=jnp.float32,
    )
    projected = lax.dot_general(
        sketched,
        sketched_rhs,
        dims,
        precision=lax.Precision.HIGHEST,
        preferred_element_type=jnp.float32,
    )
    return (gram_matrix, projected)


def solve_points(point_params, gram_matrix, projected):
    gram_blocks = gram_matrix.reshape(TERMS, K, TERMS, K)
    proj_blocks = projected.reshape(TERMS, K)
    pair_weight = point_params[:, :, None] * point_params[:, None, :]
    normal = jnp.einsum("pqr,qirj->pij", pair_weight, gram_blocks, precision=lax.Precision.HIGHEST)
    right_side = jnp.einsum("pq,qi->pi", point_params, proj_blocks, precision=lax.Precision.HIGHEST)
    lower_factor = jnp.linalg.cholesky(normal)
    forward = lax.linalg.triangular_solve(
        lower_factor, right_side[:, :, None], left_side=True, lower=True
    )
    solved = lax.linalg.triangular_solve(
        lower_factor, forward, left_side=True, lower=True, transpose_a=True
    )
    return solved[:, :, 0]


def per_device(basis, rhs, coeffs, rows, signs, params, order):
    cell_count = basis.shape[1] * basis.shape[2] * basis.shape[3]
    padded = extended(basis, (("narrow", 1), ("wide", 2)), 1).astype(jnp.float32)
    centre = padded[:, 1:-1, 1:-1, :]
    along_x = 2.0 * centre - padded[:, :-2, 1:-1, :] - padded[:, 2:, 1:-1, :]
    along_y = 2.0 * centre - padded[:, 1:-1, :-2, :] - padded[:, 1:-1, 2:, :]
    z_padded = jnp.pad(centre, ((0, 0), (0, 0), (0, 0), (1, 1)))
    along_z = 2.0 * centre - z_padded[..., :-2] - z_padded[..., 2:]
    terms = jnp.stack(
        [coeffs[0] * centre, coeffs[1] * along_x, coeffs[2] * along_y, coeffs[3] * along_z]
    )
    terms = terms.astype(jnp.bfloat16).reshape(TERMS * K, cell_count)
    row_block = M // NNZ
    flat_rows = rows.reshape(NNZ, cell_count)
    sign_values = ((2 * signs - 1).astype(jnp.float32) * 0.5).reshape(NNZ, cell_count)
    flat_rhs = rhs.reshape(cell_count)
    block_cells = max(min(1024, cell_count), cell_count // 16)
    block_count = cell_count // block_cells
    row_slots = lax.broadcasted_iota(jnp.int32, (1, row_block, 1), 1)

    def accumulate(turn_index, carry):
        sketch_sum, rhs_sum = carry
        offset = turn_index * block_cells
        hashed_rows = lax.dynamic_slice_in_dim(flat_rows, offset, block_cells, 1)
        hashed_signs = lax.dynamic_slice_in_dim(sign_values, offset, block_cells, 1)
        hashed = jnp.where(row_slots == hashed_rows[:, None, :], hashed_signs[:, None, :], 0.0)
        hashed = hashed.astype(jnp.bfloat16).reshape(M, block_cells)
        columns = lax.dynamic_slice_in_dim(terms, offset, block_cells, 1)
        sketch_sum = sketch_sum + lax.dot_general(
            hashed, columns, (((1,), (1,)), ((), ())), preferred_element_type=jnp.float32
        )
        source = lax.dynamic_slice_in_dim(flat_rhs, offset, block_cells, 0)
        rhs_sum = rhs_sum + jnp.dot(hashed, source, preferred_element_type=jnp.float32)
        return (sketch_sum, rhs_sum)

    start = (jnp.zeros((M, TERMS * K), jnp.float32), jnp.zeros((M,), jnp.float32))
    sketched, sketched_rhs = lax.fori_loop(0, block_count, accumulate, start)
    sketched, sketched_rhs = lax.psum((sketched, sketched_rhs), ("narrow", "wide"))
    gram_matrix, projected = column_products(sketched, sketched_rhs)
    own_coef = solve_points(params, gram_matrix, projected).astype(jnp.bfloat16)
    all_coef = lax.all_gather(own_coef, ("narrow", "wide"), axis=0, tiled=True)
    point_total = all_coef.shape[0]
    picker = (order[:, None] == lax.broadcasted_iota(jnp.int32, (1, point_total), 1)).astype(
        jnp.bfloat16
    )
    picked = jnp.dot(picker, all_coef, preferred_element_type=jnp.float32).astype(jnp.bfloat16)
    fields = jnp.dot(picked, basis.reshape(K, cell_count), preferred_element_type=jnp.float32)
    return fields.astype(jnp.bfloat16).reshape(
        point_total, basis.shape[1], basis.shape[2], basis.shape[3]
    )


def solution(mesh):
    in_specs = (
        P(None, "narrow", "wide", None),
        P("narrow", "wide", None),
        P(None, "narrow", "wide", None),
        P(None, "narrow", "wide", None),
        P(None, "narrow", "wide", None),
        P(("narrow", "wide"), None),
        P(),
    )
    out_specs = P(None, "narrow", "wide", None)
    return jax.shard_map(
        per_device, mesh=mesh, in_specs=in_specs, out_specs=out_specs, check_vma=False
    )
```

profile of v0, /device:TPU:1, one launch (start us, length us, event | category | flops | bytes accessed | tf_op | source)
XLA Modules:
  0.0 799.9 jit_solution(9524437281529108941)
XLA Ops:
  6.5 1.6 fusion.34
  9.0 5.1 collective-permute-start
  15.8 8.4 %collective-permute-done = bf16[128,1,16,128]{3,0,2,1:T(8,128)(2,1)} collective-permute-done((bf16[128,1,16,128]{3,0,2,1:T(8,128)(2,1)}, bf16[128,1,16,128]{3,0,2,1:T(8,128)(2,1)}, u32[]{:S(2)}, u32[]{:S(2)}) %collective-permute-start) | collective-permute-done | bytes 524320 | tf_op jit(solution)/shard_map/ppermute | solution.py:20
  25.4 1.5 constant_dynamic-update-slice_fusion.1
  26.9 10.0 %collective-permute-done.1 = bf16[128,1,16,128]{3,0,2,1:T(8,128)(2,1)S(1)} collective-permute-done((bf16[128,1,16,128]{3,0,2,1:T(8,128)(2,1)S(1)}, bf16[128,1,16,128]{3,0,2,1:T(8,128)(2,1)S(1)}, u32[]{:S(2)}, u32[]{:S(2)}) %collective-permute-start.1) | collective-permute-done | bytes 524320 | tf_op jit(solution)/shard_map/ppermute | solution.py:22
  37.0 6.3 collective-permute-start.2
  43.3 1.9 collective-permute-start.3
  46.0 7.4 collective-permute-done.3
  53.9 3.1 fusion.14
  57.0 2.2 fusion.19
  59.2 3.8 pad_maximum_fusion
  63.0 12.0 %copy.17 = bf16[4,128,4,16,128]{4,3,2,1,0:T(8,128)(2,1)} copy(bf16[4,128,4,16,128]{4,1,3,2,0:T(8,128)(2,1)} %pad_maximum_fusion) | data formatting | bytes 16777216 | tf_op jit(solution)/shard_map/stack | solution.py:72
  75.1 13.3 %convert_element_type.36 = bf16[512,8192]{1,0:T(8,128)(2,1)} reshape(bf16[4,128,4,16,128]{4,3,2,1,0:T(8,128)(2,1)} %copy.17) | data formatting | bytes 16777216 | tf_op jit(solution)/shard_map/convert_element_type | solution.py:75
  88.4 50.1 %while.16 = (s32[]{:T(128)}, f32[1024,512]{1,0:T(8,128)}, f32[1024]{0:T(1024)S(1)}, s32[4,8192]{1,0:T(4,128)S(1)}, bf16[4,8192]{1,0:T(4,128)(2,1)S(1)}, /*index=...) while((s32[]{:T(128)}, f32[1024,512]{1,0:T(8,128)}, ...), condition=%wide.region_1.2_spmd.clone, body=%wide.region_0.1_spmd.clone.sunk | while | flops 1078986752 | bytes 11651254 | solution.py:100
  88.8 3.8 select_add_fusion.4
  94.5 4.5 select_add_fusion.4
  100.8 4.5 select_add_fusion.4
  107.2 4.5 select_add_fusion.4
  113.5 4.5 select_add_fusion.4
  119.9 4.5 select_add_fusion.4
  126.2 4.5 select_add_fusion.4
  132.6 4.5 select_add_fusion.4
  138.6 78.1 %psum.15 = f32[1024]{0:T(1024)S(1)} all-reduce(f32[1024]{0:T(1024)S(1)} %get-tuple-element.146), channel_id=1, replica_groups=mesh['narrow'=8,'wide'=32] {'narrow','wide'}, use_global_device_ids=true, to_apply=%region_5.6 | all-reduce | flops 1024 | bytes 8192 | tf_op jit(solution)/shard_map/psum | solution.py:101
  216.7 186.0 %all-reduce.3.cloned.1.call-done = f32[1024,512]{1,0:T(8,128)} async-done(((f32[1024,512]{1,0:T(8,128)}), f32[1024,512]{1,0:T(8,128)}) %all-reduce.3.cloned.1.call-update) | async-done | bytes 2097168 | tf_op jit(solution)/shard_map/psum | solution.py:101
  402.7 5.7 fusion.36
  409.7 2.7 convolution_bitcast_fusion
  412.7 11.7 %custom-call.9 = f32[1,128,128]{2,1,0:T(8,128)S(1)} custom-call(f32[1,128,128]{2,1,0:T(8,128)S(1)} %fusion.29), custom_call_target="Cholesky" | custom-call | tf_op jit(solution)/shard_map/jit(cholesky)/cholesky | solution.py:54
  425.7 9.8 %custom-call.10 = f32[1,1,128,128]{2,3,1,0:T(8,128)S(1)} custom-call(f32[1,1,128,128]{3,2,1,0:T(8,128)S(1)} %fusion.24), custom_call_target="InvertDiagBlocksLowerTriangular" | custom-call | tf_op jit(solution)/shard_map/triangular_solve | solution.py:58
  435.5 1.5 fusion.37
  437.5 344.6 %all-gather.1 = bf16[256,1,128]{2,1,0:T(2,128)(2,1)S(1)} all-gather(bf16[1,1,128]{2,1,0:T(2,128)(2,1)S(1)} %fusion.21), channel_id=2, replica_groups=mesh['narrow'=8,'wide'=32] {'narrow','wide'}, dimensions={0}, use_global_device_ids=true | all-gather | bytes 65792 | tf_op jit(solution)/shard_map/all_gather | solution.py:104
  782.1 5.6 fusion.13
  787.7 5.4 copy.27
  (113 shorter events, 22.5 us)
Async XLA Ops:
  6.5 18.8 %copy-start.1 = (bf16[128,4,16,128]{3,2,1,0:T(8,128)(2,1)S(1)}, bf16[128,4,16,128]{3,2,1,0:T(8,128)(2,1)}, u32[]{:S(2)}) copy-start(bf16[128,4,16,128]{3,2,1,0:T(8,128)(2,1)} %param.9) | copy-start | bytes 6291460
  6.5 9.1 %copy-start.2 = (s32[4,4,16,128]{3,2,1,0:T(8,128)S(1)}, s32[4,4,16,128]{3,2,1,0:T(8,128)}, u32[]{:S(2)}) copy-start(s32[4,4,16,128]{3,2,1,0:T(8,128)} %param.13) | copy-start | bytes 393220
  6.5 9.2 %copy-start.3 = (s32[4,4,16,128]{3,2,1,0:T(8,128)S(1)}, s32[4,4,16,128]{3,2,1,0:T(8,128)}, u32[]{:S(2)}) copy-start(s32[4,4,16,128]{3,2,1,0:T(8,128)} %param.12) | copy-start | bytes 393220
  6.5 396.1 %all-reduce.3.cloned.1.call-start = ((), (), s32[]{:S(2)}) async-start(), calls=%async_computation | async-start | bytes 4194304 | tf_op jit(solution)/shard_map/psum | solution.py:101
  9.0 15.3 %collective-permute-start = (bf16[128,1,16,128]{3,0,2,1:T(8,128)(2,1)}, bf16[128,1,16,128]{3,0,2,1:T(8,128)(2,1)}, u32[]{:S(2)}, u32[]{:S(2)}) collective-permute-start(bf16[128,1,16,128]{3,0,2,1:T(8,128)(2,1)} %copy.40), channel_id=1, source_target_pairs={{0,32},{32,64},{64,96},{96,128},{128,160},{160,192},{192,224},{1,3... | collective-permute-start | bytes 1572872 | tf_op jit(solution)/shard_map/ppermute | solution.py:20
  14.3 22.6 %collective-permute-start.1 = (bf16[128,1,16,128]{3,0,2,1:T(8,128)(2,1)S(1)}, bf16[128,1,16,128]{3,0,2,1:T(8,128)(2,1)S(1)}, u32[]{:S(2)}, u32[]{:S(2)}) collective-permute-start(bf16[128,1,16,128]{3,0,2,1:T(8,128)(2,1)S(1)} %copy.41), channel_id=1, source_target_pairs={{32,0},{64,32},{96,64},{128,96},{160,128},{192,160},{224,192},{33,... | collective-permute-start | bytes 1572872 | tf_op jit(solution)/shard_map/ppermute | solution.py:22
  25.4 19.9 %copy-start.4 = (f32[4,4,16,128]{3,2,1,0:T(8,128)S(1)}, f32[4,4,16,128]{3,2,1,0:T(8,128)}, u32[]{:S(2)}) copy-start(f32[4,4,16,128]{3,2,1,0:T(8,128)} %param.11) | copy-start | bytes 393220
  37.0 8.9 %collective-permute-start.2 = (bf16[128,6,1,128]{3,0,2,1:T(8,128)(2,1)S(1)}, bf16[128,6,1,128]{3,0,2,1:T(8,128)(2,1)S(1)}, u32[]{:S(2)}, u32[]{:S(2)}) collective-permute-start(bf16[128,6,1,128]{3,0,2,1:T(8,128)(2,1)S(1)} %get-tuple-element.191), channel_id=1, source_target_pairs={{0,1},{1,2},{2,3},{3,4},{4,5},{5,6},{6,7},{7,8},{8,9},{9,10},{10,1... | collective-permute-start | bytes 589832 | tf_op jit(solution)/shard_map/ppermute | solution.py:20
  43.3 10.0 %collective-permute-start.3 = (bf16[128,6,1,128]{3,0,2,1:T(8,128)(2,1)S(1)}, bf16[128,6,1,128]{3,0,2,1:T(8,128)(2,1)S(1)}, u32[]{:S(2)}, u32[]{:S(2)}) collective-permute-start(bf16[128,6,1,128]{3,0,2,1:T(8,128)(2,1)S(1)} %get-tuple-element.192), channel_id=1, source_target_pairs={{1,0},{2,1},{3,2},{4,3},{5,4},{6,5},{7,6},{8,7},{9,8},{10,9},{11,1... | collective-permute-start | bytes 589832 | tf_op jit(solution)/shard_map/ppermute | solution.py:22
  88.4 50.1 %copy-start.5 = (f32[1,4]{1,0:T(1,128)S(1)}, f32[1,4]{1,0:T(1,128)}, u32[]{:S(2)}) copy-start(f32[1,4]{1,0:T(1,128)} %param.14) | copy-start | bytes 52
  408.4 27.2 %copy-start = (f32[1024,512]{1,0:T(8,128)S(1)}, f32[1024,512]{1,0:T(8,128)}, u32[]{:S(2)}) copy-start(f32[1024,512]{1,0:T(8,128)} %all-reduce.3.cloned.1.call-done) | copy-start | bytes 6291460
  408.4 373.7 %copy-start.6 = (s32[256]{0:T(256)S(1)}, s32[256]{0:T(256)}, u32[]{:S(2)}) copy-start(s32[256]{0:T(256)} %param.15) | copy-start | bytes 3076
Sparse Core Ops, SparseCore 0:
  138.6 263.9 all-reduce.2
where the time goes:
time: 801 us; the launch traced here: 800 us
  blocking collectives  423 us (53%)
  waiting for transfers between devices  213 us (27%)
  matrix products  56.7 us (7%)
  local copies, waits for them, and re-layouts  43.4 us (5%)
  other arithmetic  36 us (4%)
  starting transfers between devices  14.7 us (2%)
  between operations  13.6 us (2%)
    all_gather x1, blocking collectives, per_device(): all_coef = lax.all_gather(own_coef, ('narrow', 'wide'), axis=0, tiled=True)  345 us
    psum x1, waiting for transfers between devices, per_device(): lax.psum((sketched, sketched_rhs), ('narrow', 'wide'))  186 us
    psum x1, blocking collectives, per_device(): lax.psum((sketched, sketched_rhs), ('narrow', 'wide'))  78.1 us
    dot_general x8, matrix products, accumulate(): lax.dot_general(hashed, columns, (((1,), (1,)), ((), ())), preferred_elem...  35.6 us
    ppermute x2, waiting for transfers between devices, extended(): lax.ppermute(head, axis, [((i + 1) % count, i) for i in range(ends)])  17.4 us
  transfers between devices with their start and end apart: 5, of which 5 were waited for; matrix products, arithmetic and copies ran while one was open for 0% of the time, Pallas kernels for 0%

commit v1 on v0

--- a/solution.py
+++ b/solution.py
@@ -101,7 +101,12 @@
     sketched, sketched_rhs = lax.psum((sketched, sketched_rhs), ("narrow", "wide"))
     gram_matrix, projected = column_products(sketched, sketched_rhs)
     own_coef = solve_points(params, gram_matrix, projected).astype(jnp.bfloat16)
-    all_coef = lax.all_gather(own_coef, ("narrow", "wide"), axis=0, tiled=True)
+    all_coef = jnp.concatenate(
+        lax.all_to_all(
+            jnp.stack([own_coef] * lax.axis_size(("narrow", "wide"))), ("narrow", "wide"), 0, 0
+        ),
+        axis=0,
+    )
     point_total = all_coef.shape[0]
     picker = (order[:, None] == lax.broadcasted_iota(jnp.int32, (1, point_total), 1)).astype(
         jnp.bfloat16

time: 801 us -> 482 us (0.60)
  blocking collectives: 423 us -> 103 us
    all_gather x1 -> x0, blocking collectives: 345 us -> none  [per_device(): all_coef = lax.all_gather(own_coef, ('narrow', 'wide'), axis=0, tiled=True)]
    all_to_all x0 -> x1, blocking collectives: none -> 25 us  [per_device(): lax.all_to_all(jnp.stack([own_coef] * lax.axis_size(('narrow', 'wide'))),...]
  transfers between devices with their start and end apart: 5 -> 5, of which waited for: 5 -> 5; matrix products, arithmetic and copies ran while one was open for 0% -> 1% of each run, Pallas kernels for 0% -> 0%
where the time goes in v1:
time: 482 us; the launch traced here: 480 us
  waiting for transfers between devices  213 us (44%)
  blocking collectives  103 us (21%)
  matrix products  56.7 us (12%)
  local copies, waits for them, and re-layouts  43.5 us (9%)
  other arithmetic  36 us (7%)
  starting transfers between devices  14.7 us (3%)
  between operations  13.7 us (3%)
    psum x1, waiting for transfers between devices, per_device(): lax.psum((sketched, sketched_rhs), ('narrow', 'wide'))  186 us
    psum x1, blocking collectives, per_device(): lax.psum((sketched, sketched_rhs), ('narrow', 'wide'))  78.1 us
    dot_general x8, matrix products, accumulate(): lax.dot_general(hashed, columns, (((1,), (1,)), ((), ())), preferred_elem...  35.6 us
    all_to_all x1, blocking collectives, per_device(): lax.all_to_all(jnp.stack([own_coef] * lax.axis_size(('narrow', 'wide'))),...  25 us
    ppermute x2, waiting for transfers between devices, extended(): lax.ppermute(head, axis, [((i + 1) % count, i) for i in range(ends)])  17.4 us
    convert_element_type x1, local copies, waits for them, and re-layouts, per_device(): terms = terms.astype(jnp.bfloat16).reshape(TERMS * K, cell_count)  13.3 us
    another operation x3, other arithmetic, solve_points(): lower_factor = jnp.linalg.cholesky(normal)  12.4 us
    another operation x1, local copies, waits for them, and re-layouts, per_device(): jnp.stack([coeffs[0] * centre, coeffs[1] * along_x, coeffs[2] * along_y,...  12 us
  transfers between devices with their start and end apart: 5, of which 5 were waited for; matrix products, arithmetic and copies ran while one was open for 1% of the time, Pallas kernels for 0%

profile of v1, /device:TPU:1, one launch (start us, length us, event | category | flops | bytes accessed | tf_op | source)
XLA Modules:
  0.0 480.5 jit_solution(15964447661283054262)
XLA Ops:
  6.5 1.6 fusion.33
  9.0 5.1 %collective-permute-start = (bf16[128,1,16,128]{3,0,2,1:T(8,128)(2,1)}, bf16[128,1,16,128]{3,0,2,1:T(8,128)(2,1)}, u32[]{:S(2)}, u32[]{:S(2)}) collective-permute-start(bf16[128,1,16,128]{3,0,2,1:T(8,128)(2,1)} %copy.40), channel_id=1, source_target_pairs={{0,32},{32,64},{64,96},{96,128},{128,160},{160,192},{192,224},{1,3... | collective-permute-start | bytes 1572872 | tf_op jit(solution)/shard_map/ppermute | solution.py:20
  15.8 8.4 %collective-permute-done = bf16[128,1,16,128]{3,0,2,1:T(8,128)(2,1)} collective-permute-done((bf16[128,1,16,128]{3,0,2,1:T(8,128)(2,1)}, bf16[128,1,16,128]{3,0,2,1:T(8,128)(2,1)}, u32[]{:S(2)}, u32[]{:S(2)}) %collective-permute-start) | collective-permute-done | bytes 524320 | tf_op jit(solution)/shard_map/ppermute | solution.py:20
  25.4 1.5 constant_dynamic-update-slice_fusion.1
  26.9 10.0 %collective-permute-done.1 = bf16[128,1,16,128]{3,0,2,1:T(8,128)(2,1)S(1)} collective-permute-done((bf16[128,1,16,128]{3,0,2,1:T(8,128)(2,1)S(1)}, bf16[128,1,16,128]{3,0,2,1:T(8,128)(2,1)S(1)}, u32[]{:S(2)}, u32[]{:S(2)}) %collective-permute-start.1) | collective-permute-done | bytes 524320 | tf_op jit(solution)/shard_map/ppermute | solution.py:22
  37.0 6.3 %collective-permute-start.2 = (bf16[128,6,1,128]{3,0,2,1:T(8,128)(2,1)S(1)}, bf16[128,6,1,128]{3,0,2,1:T(8,128)(2,1)S(1)}, u32[]{:S(2)}, u32[]{:S(2)}) collective-permute-start(bf16[128,6,1,128]{3,0,2,1:T(8,128)(2,1)S(1)} %get-tuple-element.191), channel_id=1, source_target_pairs={{0,1},{1,2},{2,3},{3,4},{4,5},{5,6},{6,7},{7,8},{8,9},{9,10},{10,1... | collective-permute-start | bytes 589832 | tf_op jit(solution)/shard_map/ppermute | solution.py:20
  43.3 1.9 collective-permute-start.3
  46.0 7.4 %collective-permute-done.3 = bf16[128,6,1,128]{3,0,2,1:T(8,128)(2,1)S(1)} collective-permute-done((bf16[128,6,1,128]{3,0,2,1:T(8,128)(2,1)S(1)}, bf16[128,6,1,128]{3,0,2,1:T(8,128)(2,1)S(1)}, u32[]{:S(2)}, u32[]{:S(2)}) %collective-permute-start.3) | collective-permute-done | bytes 196640 | tf_op jit(solution)/shard_map/ppermute | solution.py:22
  53.9 3.1 fusion.14
  57.0 2.2 fusion.19
  59.2 3.8 pad_maximum_fusion
  63.0 12.0 %copy.17 = bf16[4,128,4,16,128]{4,3,2,1,0:T(8,128)(2,1)} copy(bf16[4,128,4,16,128]{4,1,3,2,0:T(8,128)(2,1)} %pad_maximum_fusion) | data formatting | bytes 16777216 | tf_op jit(solution)/shard_map/stack | solution.py:72
  75.1 13.3 %convert_element_type.34 = bf16[512,8192]{1,0:T(8,128)(2,1)} reshape(bf16[4,128,4,16,128]{4,3,2,1,0:T(8,128)(2,1)} %copy.17) | data formatting | bytes 16777216 | tf_op jit(solution)/shard_map/convert_element_type | solution.py:75
  88.4 50.1 %while.16 = (s32[]{:T(128)}, f32[1024,512]{1,0:T(8,128)}, f32[1024]{0:T(1024)S(1)}, s32[4,8192]{1,0:T(4,128)S(1)}, bf16[4,8192]{1,0:T(4,128)(2,1)S(1)}, /*index=...) while((s32[]{:T(128)}, f32[1024,512]{1,0:T(8,128)}, ...), condition=%wide.region_1.2_spmd.clone, body=%wide.region_0.1_spmd.clone.sunk | while | flops 1078986752 | bytes 11651254 | solution.py:100
  88.8 3.8 select_add_fusion.4
  94.5 4.5 select_add_fusion.4
  100.8 4.5 select_add_fusion.4
  107.2 4.5 select_add_fusion.4
  113.5 4.5 select_add_fusion.4
  119.9 4.5 select_add_fusion.4
  126.2 4.5 select_add_fusion.4
  132.6 4.5 select_add_fusion.4
  138.6 78.1 %psum.15 = f32[1024]{0:T(1024)S(1)} all-reduce(f32[1024]{0:T(1024)S(1)} %get-tuple-element.146), channel_id=1, replica_groups=mesh['narrow'=8,'wide'=32] {'narrow','wide'}, use_global_device_ids=true, to_apply=%region_5.6 | all-reduce | flops 1024 | bytes 8192 | tf_op jit(solution)/shard_map/psum | solution.py:101
  216.7 186.0 %all-reduce.3.cloned.1.call-done = f32[1024,512]{1,0:T(8,128)} async-done(((f32[1024,512]{1,0:T(8,128)}), f32[1024,512]{1,0:T(8,128)}) %all-reduce.3.cloned.1.call-update) | async-done | bytes 2097168 | tf_op jit(solution)/shard_map/psum | solution.py:101
  402.7 5.7 %fusion.35 = f32[512,512]{1,0:T(8,128)S(1)} fusion(f32[1024,512]{1,0:T(8,128)} %all-reduce.3.cloned.1.call-done), kind=kOutput, calls=%fused_computation.71 | convolution fusion | flops 3221225472 | bytes 3145728 | tf_op jit(solution)/shard_map/dot_general | solution.py:31
  409.7 2.7 convolution_bitcast_fusion
  412.7 11.7 %custom-call.9 = f32[1,128,128]{2,1,0:T(8,128)S(1)} custom-call(f32[1,128,128]{2,1,0:T(8,128)S(1)} %fusion.28), custom_call_target="Cholesky" | custom-call | tf_op jit(solution)/shard_map/jit(cholesky)/cholesky | solution.py:54
  425.7 9.8 %custom-call.10 = f32[1,1,128,128]{2,3,1,0:T(8,128)S(1)} custom-call(f32[1,1,128,128]{3,2,1,0:T(8,128)S(1)} %fusion.23), custom_call_target="InvertDiagBlocksLowerTriangular" | custom-call | tf_op jit(solution)/shard_map/triangular_solve | solution.py:58
  435.5 1.5 fusion.36
  437.6 25.0 %all_to_all.5 = bf16[256,1,128]{2,1,0:T(2,128)(2,1)S(1)} all-to-all(bf16[256,1,128]{2,1,0:T(2,128)(2,1)S(1)} %stack.22), channel_id=1, replica_groups=mesh['narrow'=8,'wide'=32] {'narrow','wide'}, dimensions={0} | all-to-all | bytes 131072 | tf_op jit(solution)/shard_map/all_to_all | solution.py:105
  462.6 5.6 %fusion.13 = bf16[32,8,64,128]{3,1,2,0:T(8,128)(2,1)} fusion(bf16[16,8,64,128]{3,2,1,0:T(8,128)(2,1)} %bitcast.124, s32[256]{0:T(256)S(1)} %copy-done.6, bf16[256,1,128]{2,1,0:T(2,128)(2,1)S(1)} %all_to_all.5), kind=kOutput, calls=%fused_computation.29 | convolution fusion | flops 555843584 | bytes 6358016 | tf_op jit(solution)/shard_map/dot_general | solution.py:115
  468.2 5.4 %copy.27 = bf16[32,8,64,128]{3,2,1,0:T(8,128)(2,1)} copy(bf16[32,8,64,128]{3,1,2,0:T(8,128)(2,1)} %fusion.13) | data formatting | bytes 8388608
  (114 shorter events, 22.7 us)
Async XLA Ops:
  6.5 18.8 %copy-start.1 = (bf16[128,4,16,128]{3,2,1,0:T(8,128)(2,1)S(1)}, bf16[128,4,16,128]{3,2,1,0:T(8,128)(2,1)}, u32[]{:S(2)}) copy-start(bf16[128,4,16,128]{3,2,1,0:T(8,128)(2,1)} %param.9) | copy-start | bytes 6291460
  6.5 9.1 %copy-start.2 = (s32[4,4,16,128]{3,2,1,0:T(8,128)S(1)}, s32[4,4,16,128]{3,2,1,0:T(8,128)}, u32[]{:S(2)}) copy-start(s32[4,4,16,128]{3,2,1,0:T(8,128)} %param.13) | copy-start | bytes 393220
  6.5 9.2 %copy-start.3 = (s32[4,4,16,128]{3,2,1,0:T(8,128)S(1)}, s32[4,4,16,128]{3,2,1,0:T(8,128)}, u32[]{:S(2)}) copy-start(s32[4,4,16,128]{3,2,1,0:T(8,128)} %param.12) | copy-start | bytes 393220
  6.5 396.1 %all-reduce.3.cloned.1.call-start = ((), (), s32[]{:S(2)}) async-start(), calls=%async_computation.1 | async-start | bytes 4194304 | tf_op jit(solution)/shard_map/psum | solution.py:101
  9.0 15.3 %collective-permute-start = (bf16[128,1,16,128]{3,0,2,1:T(8,128)(2,1)}, bf16[128,1,16,128]{3,0,2,1:T(8,128)(2,1)}, u32[]{:S(2)}, u32[]{:S(2)}) collective-permute-start(bf16[128,1,16,128]{3,0,2,1:T(8,128)(2,1)} %copy.40), channel_id=1, source_target_pairs={{0,32},{32,64},{64,96},{96,128},{128,160},{160,192},{192,224},{1,3... | collective-permute-start | bytes 1572872 | tf_op jit(solution)/shard_map/ppermute | solution.py:20
  14.3 22.6 %collective-permute-start.1 = (bf16[128,1,16,128]{3,0,2,1:T(8,128)(2,1)S(1)}, bf16[128,1,16,128]{3,0,2,1:T(8,128)(2,1)S(1)}, u32[]{:S(2)}, u32[]{:S(2)}) collective-permute-start(bf16[128,1,16,128]{3,0,2,1:T(8,128)(2,1)S(1)} %copy.41), channel_id=1, source_target_pairs={{32,0},{64,32},{96,64},{128,96},{160,128},{192,160},{224,192},{33,... | collective-permute-start | bytes 1572872 | tf_op jit(solution)/shard_map/ppermute | solution.py:22
  25.4 19.9 %copy-start.4 = (f32[4,4,16,128]{3,2,1,0:T(8,128)S(1)}, f32[4,4,16,128]{3,2,1,0:T(8,128)}, u32[]{:S(2)}) copy-start(f32[4,4,16,128]{3,2,1,0:T(8,128)} %param.11) | copy-start | bytes 393220
  37.0 8.9 %collective-permute-start.2 = (bf16[128,6,1,128]{3,0,2,1:T(8,128)(2,1)S(1)}, bf16[128,6,1,128]{3,0,2,1:T(8,128)(2,1)S(1)}, u32[]{:S(2)}, u32[]{:S(2)}) collective-permute-start(bf16[128,6,1,128]{3,0,2,1:T(8,128)(2,1)S(1)} %get-tuple-element.191), channel_id=1, source_target_pairs={{0,1},{1,2},{2,3},{3,4},{4,5},{5,6},{6,7},{7,8},{8,9},{9,10},{10,1... | collective-permute-start | bytes 589832 | tf_op jit(solution)/shard_map/ppermute | solution.py:20
  43.3 10.0 %collective-permute-start.3 = (bf16[128,6,1,128]{3,0,2,1:T(8,128)(2,1)S(1)}, bf16[128,6,1,128]{3,0,2,1:T(8,128)(2,1)S(1)}, u32[]{:S(2)}, u32[]{:S(2)}) collective-permute-start(bf16[128,6,1,128]{3,0,2,1:T(8,128)(2,1)S(1)} %get-tuple-element.192), channel_id=1, source_target_pairs={{1,0},{2,1},{3,2},{4,3},{5,4},{6,5},{7,6},{8,7},{9,8},{10,9},{11,1... | collective-permute-start | bytes 589832 | tf_op jit(solution)/shard_map/ppermute | solution.py:22
  88.4 50.1 %copy-start.5 = (f32[1,4]{1,0:T(1,128)S(1)}, f32[1,4]{1,0:T(1,128)}, u32[]{:S(2)}) copy-start(f32[1,4]{1,0:T(1,128)} %param.14) | copy-start | bytes 52
  408.4 27.2 %copy-start = (f32[1024,512]{1,0:T(8,128)S(1)}, f32[1024,512]{1,0:T(8,128)}, u32[]{:S(2)}) copy-start(f32[1024,512]{1,0:T(8,128)} %all-reduce.3.cloned.1.call-done) | copy-start | bytes 6291460
  408.4 54.3 %copy-start.6 = (s32[256]{0:T(256)S(1)}, s32[256]{0:T(256)}, u32[]{:S(2)}) copy-start(s32[256]{0:T(256)} %param.15) | copy-start | bytes 3076
Sparse Core Ops, SparseCore 0:
  138.6 263.9 all-reduce.2
